TPU v7x, 256 devices: a whole 4x4x8 slice. The times are simulated.
256 devices in a mesh: section: 16 (over z, y_lo), tile: 16 (over x, y_hi, core).
Axes of the slice: x: 4, y: 4 (y_hi: 2, y_lo: 2; y = y_hi * 2 + y_lo), z: 8, core: 2. Of those that a mesh axis runs over, the one named last changes fastest.
Arguments:
- acts: bfloat16 [16, 2, 256, 128, 128], P('section', None, None, 'tile'), may hold values from -6 to 6
- weights: bfloat16 [16, 9, 256, 256], P('section'), may hold values from -0.0625 to 0.0625
- cotangent: bfloat16 [2, 256, 128, 128], P(None, None, 'tile'), may hold values from -6 to 6
Outputs:
- grad_acts: bfloat16 [16, 2, 256, 128, 128], P('section', None, None, 'tile')
- weight_grad: float32 [16, 9, 256, 256], P('section')
All inputs are finite; a program needn't handle non-finite values.
Results may differ from a plain program's by a relative error of at most 0.017.
Values may be sent and summed in bfloat16 or wider, within the bound.
No kernel may reach another device: no remote copies, remote signals or barrier semaphores. Data moves between devices by JAX's collectives and lax.ppermute only.
A program may use at most 64 MiB of HBM per device.

v0:
```python
import jax
import jax.numpy as jnp
from jax import lax
from jax.sharding import PartitionSpec as P


def padded_2(block, sides, width):
    for axis, dim in sides:
        count = lax.axis_size(axis)
        forward = [(i, i + 1) for i in range(count - 1)]
        forward.append((count - 1, 0))
        backward = [(target, source) for source, target in forward]
        low = lax.ppermute(
            lax.slice_in_dim(block, block.shape[dim] - width, None, axis=dim), axis, forward
        )
        high = lax.ppermute(lax.slice_in_dim(block, 0, width, axis=dim), axis, backward)
        block = jnp.concatenate([low, block, high], axis=dim)
    return block


def from_behind(block, axis, distance):
    devices = range(lax.axis_size(axis))
    route = [(i - distance, i) for i in devices if i - distance in devices]
    return lax.ppermute(block, axis, route)


def shift_cols(field, offset):
    if offset == 0:
        return field
    zeros = jnp.zeros_like(field[..., :1])
    if offset == 1:
        return jnp.concatenate([field[..., 1:], zeros], axis=-1)
    return jnp.concatenate([zeros, field[..., :-1]], axis=-1)


def back_conv(padded, kernel, height):
    total = jnp.zeros(padded.shape[:2] + (height, padded.shape[3]), jnp.float32)
    for row_step in (-1, 0, 1):
        rows_cut = padded[:, :, 1 - row_step : 1 - row_step + height, :]
        for col_step in (-1, 0, 1):
            index = (row_step + 1) * 3 + col_step + 1
            moved = shift_cols(rows_cut, -col_step)
            total = total + jnp.einsum(
                "oi,gorc->girc", kernel[index], moved, preferred_element_type=jnp.float32
            )
    return total


def kernel_grad(padded, hidden_rims, height):
    grad_mid = padded[:, :, 1 : 1 + height, :]
    parts = []
    for row_step in (-1, 0, 1):
        rows_cut = hidden_rims[:, :, 1 + row_step : 1 + row_step + height, :]
        for col_step in (-1, 0, 1):
            seen = shift_cols(rows_cut, col_step)
            parts.append(
                jnp.einsum("gorc,girc->oi", grad_mid, seen, preferred_element_type=jnp.float32)
            )
    return jnp.stack(parts)


def per_device(acts, weights, cotangent):
    n_section = lax.axis_size("section")
    section_id = lax.axis_index("section")
    inputs = acts[0].astype(jnp.float32)
    kernel = weights[0]
    batches, chans, height, width = acts.shape[1:]
    sigma = jax.nn.sigmoid(inputs)
    hidden = (inputs * sigma).astype(jnp.bfloat16)
    slope = sigma * (1.0 + inputs * (1.0 - sigma))
    hidden_rims = padded_2(hidden, (("tile", 2),), 1)
    scale = 1.0 / jnp.sqrt(jnp.float32(batches * height * lax.axis_size("tile") * width))
    n_groups = batches // batches
    ticks = n_section + n_groups - 1

    def one_tick(carry, tick):
        incoming, grads, kernel_acc, stored = carry
        batch_id = tick - (n_section - 1 - section_id)
        valid = jnp.logical_and(batch_id >= 0, batch_id < n_groups)
        upper = jnp.where(section_id == n_section - 1, cotangent, incoming)
        padded = padded_2(upper, (("tile", 2),), 1)

        def active(operands):
            padded_in, upper_in, slope_in, rims_in = operands
            back = back_conv(padded_in, kernel, height)
            lowered = (upper_in.astype(jnp.float32) + back * slope_in).astype(jnp.bfloat16)
            partial_k = kernel_grad(padded_in, rims_in, height)
            return (lowered, partial_k)

        def resting(operands):
            return (jnp.zeros(upper.shape, jnp.bfloat16), jnp.zeros(kernel_acc.shape, jnp.float32))

        lowered, partial_k = lax.cond(valid, active, resting, (padded, upper, slope, hidden_rims))
        kernel_acc = kernel_acc + partial_k
        old_grads = grads
        grads = jnp.where(valid, lowered, old_grads)
        old_store = stored
        stored = jnp.where(valid, padded, old_store)
        outgoing = from_behind(lowered, "section", -1)
        return ((outgoing, grads, kernel_acc, stored), None)

    initial = (
        jnp.zeros((batches, chans, height, width), jnp.bfloat16),
        jnp.zeros((batches, chans, height, width), jnp.bfloat16),
        jnp.zeros((9, chans, chans), jnp.float32),
        jnp.zeros((batches, chans, height + 2, width), jnp.bfloat16),
    )
    final, unused = lax.scan(one_tick, initial, jnp.arange(ticks, dtype=jnp.int32))
    grads = final[1]
    kernel_acc = final[2]
    weight_grad = lax.psum(kernel_acc * scale, "tile")
    return (grads[None], weight_grad[None])


def solution(mesh):
    placed = (
        P("section", None, None, "tile", None),
        P("section", None, None, None),
        P(None, None, "tile", None),
    )
    return jax.shard_map(
        per_device,
        mesh=mesh,
        in_specs=placed,
        out_specs=(P("section", None, None, "tile", None), P("section", None, None, None)),
        check_vma=False,
    )
```

profile of v0, /device:TPU:1, one launch (start us, length us, event | category | flops | bytes accessed | tf_op | source)
XLA Modules:
  0.0 1089.7 jit_solution(17540240250807122509)
XLA Ops:
  23.7 900.9 %while.17 = (s32[]{:T(128)}, bf16[2,256,8,128]{1,3,2,0:T(8,128)(2,1)}, bf16[2,256,8,128]{1,3,2,0:T(8,128)(2,1)}, f32[9,256,256]{1,2,0:T(8,128)}, s32[16]{0:T(128...) while((s32[]{:T(128)}, ...), condition=%wide.region_3.4_spmd.clone, body=%wide.region_0.3_spmd.clone.sunk | while | flops 4842192896 | bytes 153502240 | solution.py:108
  41.6 13.8 %collective-permute-done.2 = bf16[2,256,8,128]{1,3,2,0:T(8,128)(2,1)S(1)} collective-permute-done((bf16[2,256,8,128]{1,3,2,0:T(8,128)(2,1)}, bf16[2,256,8,128]{1,3,2,0:T(8,128)(2,1)S(1)}, u32[]{:S(2)}, u32[]{:S(2)}) %collective-permute-start.2) | collective-permute-done | bytes 1048608 | tf_op jit(solution)/shard_map/while/body/eval_jaxpr/ppermute | solution.py:24
  58.4 8.1 collective-permute-start
  82.0 13.3 %collective-permute-done.2 = bf16[2,256,8,128]{1,3,2,0:T(8,128)(2,1)S(1)} collective-permute-done((bf16[2,256,8,128]{1,3,2,0:T(8,128)(2,1)}, bf16[2,256,8,128]{1,3,2,0:T(8,128)(2,1)S(1)}, u32[]{:S(2)}, u32[]{:S(2)}) %collective-permute-start.2) | collective-permute-done | bytes 1048608 | tf_op jit(solution)/shard_map/while/body/eval_jaxpr/ppermute | solution.py:24
  98.4 8.1 collective-permute-start
  122.2 14.2 %collective-permute-done.2 = bf16[2,256,8,128]{1,3,2,0:T(8,128)(2,1)S(1)} collective-permute-done((bf16[2,256,8,128]{1,3,2,0:T(8,128)(2,1)}, bf16[2,256,8,128]{1,3,2,0:T(8,128)(2,1)S(1)}, u32[]{:S(2)}, u32[]{:S(2)}) %collective-permute-start.2) | collective-permute-done | bytes 1048608 | tf_op jit(solution)/shard_map/while/body/eval_jaxpr/ppermute | solution.py:24
  139.4 7.8 collective-permute-start
  163.6 14.5 %collective-permute-done.2 = bf16[2,256,8,128]{1,3,2,0:T(8,128)(2,1)S(1)} collective-permute-done((bf16[2,256,8,128]{1,3,2,0:T(8,128)(2,1)}, bf16[2,256,8,128]{1,3,2,0:T(8,128)(2,1)S(1)}, u32[]{:S(2)}, u32[]{:S(2)}) %collective-permute-start.2) | collective-permute-done | bytes 1048608 | tf_op jit(solution)/shard_map/while/body/eval_jaxpr/ppermute | solution.py:24
  181.1 6.9 collective-permute-start
  205.3 17.4 %collective-permute-done.2 = bf16[2,256,8,128]{1,3,2,0:T(8,128)(2,1)S(1)} collective-permute-done((bf16[2,256,8,128]{1,3,2,0:T(8,128)(2,1)}, bf16[2,256,8,128]{1,3,2,0:T(8,128)(2,1)S(1)}, u32[]{:S(2)}, u32[]{:S(2)}) %collective-permute-start.2) | collective-permute-done | bytes 1048608 | tf_op jit(solution)/shard_map/while/body/eval_jaxpr/ppermute | solution.py:24
  245.3 17.5 %collective-permute-done.2 = bf16[2,256,8,128]{1,3,2,0:T(8,128)(2,1)S(1)} collective-permute-done((bf16[2,256,8,128]{1,3,2,0:T(8,128)(2,1)}, bf16[2,256,8,128]{1,3,2,0:T(8,128)(2,1)S(1)}, u32[]{:S(2)}, u32[]{:S(2)}) %collective-permute-start.2) | collective-permute-done | bytes 1048608 | tf_op jit(solution)/shard_map/while/body/eval_jaxpr/ppermute | solution.py:24
  284.6 16.7 %collective-permute-done.2 = bf16[2,256,8,128]{1,3,2,0:T(8,128)(2,1)S(1)} collective-permute-done((bf16[2,256,8,128]{1,3,2,0:T(8,128)(2,1)}, bf16[2,256,8,128]{1,3,2,0:T(8,128)(2,1)S(1)}, u32[]{:S(2)}, u32[]{:S(2)}) %collective-permute-start.2) | collective-permute-done | bytes 1048608 | tf_op jit(solution)/shard_map/while/body/eval_jaxpr/ppermute | solution.py:24
  323.9 16.6 %collective-permute-done.2 = bf16[2,256,8,128]{1,3,2,0:T(8,128)(2,1)S(1)} collective-permute-done((bf16[2,256,8,128]{1,3,2,0:T(8,128)(2,1)}, bf16[2,256,8,128]{1,3,2,0:T(8,128)(2,1)S(1)}, u32[]{:S(2)}, u32[]{:S(2)}) %collective-permute-start.2) | collective-permute-done | bytes 1048608 | tf_op jit(solution)/shard_map/while/body/eval_jaxpr/ppermute | solution.py:24
  363.0 16.5 %collective-permute-done.2 = bf16[2,256,8,128]{1,3,2,0:T(8,128)(2,1)S(1)} collective-permute-done((bf16[2,256,8,128]{1,3,2,0:T(8,128)(2,1)}, bf16[2,256,8,128]{1,3,2,0:T(8,128)(2,1)S(1)}, u32[]{:S(2)}, u32[]{:S(2)}) %collective-permute-start.2) | collective-permute-done | bytes 1048608 | tf_op jit(solution)/shard_map/while/body/eval_jaxpr/ppermute | solution.py:24
  402.0 16.5 %collective-permute-done.2 = bf16[2,256,8,128]{1,3,2,0:T(8,128)(2,1)S(1)} collective-permute-done((bf16[2,256,8,128]{1,3,2,0:T(8,128)(2,1)}, bf16[2,256,8,128]{1,3,2,0:T(8,128)(2,1)S(1)}, u32[]{:S(2)}, u32[]{:S(2)}) %collective-permute-start.2) | collective-permute-done | bytes 1048608 | tf_op jit(solution)/shard_map/while/body/eval_jaxpr/ppermute | solution.py:24
  441.1 17.7 %collective-permute-done.2 = bf16[2,256,8,128]{1,3,2,0:T(8,128)(2,1)S(1)} collective-permute-done((bf16[2,256,8,128]{1,3,2,0:T(8,128)(2,1)}, bf16[2,256,8,128]{1,3,2,0:T(8,128)(2,1)S(1)}, u32[]{:S(2)}, u32[]{:S(2)}) %collective-permute-start.2) | collective-permute-done | bytes 1048608 | tf_op jit(solution)/shard_map/while/body/eval_jaxpr/ppermute | solution.py:24
  482.0 17.2 %collective-permute-done.2 = bf16[2,256,8,128]{1,3,2,0:T(8,128)(2,1)S(1)} collective-permute-done((bf16[2,256,8,128]{1,3,2,0:T(8,128)(2,1)}, bf16[2,256,8,128]{1,3,2,0:T(8,128)(2,1)S(1)}, u32[]{:S(2)}, u32[]{:S(2)}) %collective-permute-start.2) | collective-permute-done | bytes 1048608 | tf_op jit(solution)/shard_map/while/body/eval_jaxpr/ppermute | solution.py:24
  522.5 17.0 %collective-permute-done.2 = bf16[2,256,8,128]{1,3,2,0:T(8,128)(2,1)S(1)} collective-permute-done((bf16[2,256,8,128]{1,3,2,0:T(8,128)(2,1)}, bf16[2,256,8,128]{1,3,2,0:T(8,128)(2,1)S(1)}, u32[]{:S(2)}, u32[]{:S(2)}) %collective-permute-start.2) | collective-permute-done | bytes 1048608 | tf_op jit(solution)/shard_map/while/body/eval_jaxpr/ppermute | solution.py:24
  562.8 16.8 %collective-permute-done.2 = bf16[2,256,8,128]{1,3,2,0:T(8,128)(2,1)S(1)} collective-permute-done((bf16[2,256,8,128]{1,3,2,0:T(8,128)(2,1)}, bf16[2,256,8,128]{1,3,2,0:T(8,128)(2,1)S(1)}, u32[]{:S(2)}, u32[]{:S(2)}) %collective-permute-start.2) | collective-permute-done | bytes 1048608 | tf_op jit(solution)/shard_map/while/body/eval_jaxpr/ppermute | solution.py:24
  602.8 263.3 %collective-permute-done.2 = bf16[2,256,8,128]{1,3,2,0:T(8,128)(2,1)S(1)} collective-permute-done((bf16[2,256,8,128]{1,3,2,0:T(8,128)(2,1)}, bf16[2,256,8,128]{1,3,2,0:T(8,128)(2,1)S(1)}, u32[]{:S(2)}, u32[]{:S(2)}) %collective-permute-start.2) | collective-permute-done | bytes 1048608 | tf_op jit(solution)/shard_map/while/body/eval_jaxpr/ppermute | solution.py:24
  869.2 6.7 collective-permute-start
  880.7 20.9 %conditional.3 = (bf16[2,256,8,128]{1,3,2,0:T(8,128)(2,1)}, f32[9,256,256]{1,2,0:T(8,128)}) conditional(s32[]{:T(128)} %convert_element_type.29, () %tuple.63, (bf16[2,256,8,128]{1,3,2,0:T(8,128)(2,1)S(1)}, bf16[2,256,10,128]{1,3,2,0:T(8,128)(2,1)S(1)}, bf16[9,256,256]{2,1,0:T(8,128)(2,1)}, f32[2,256,8,128]{1,3,2,0:T(8,128)S(1)}, ...), branch_computations={%region_1.1_spmd, %region_2.2_spmd} | conditional | flops 4838129664 | bytes 100286512 | solution.py:93
  908.1 15.6 %collective-permute-done.2 = bf16[2,256,8,128]{1,3,2,0:T(8,128)(2,1)S(1)} collective-permute-done((bf16[2,256,8,128]{1,3,2,0:T(8,128)(2,1)}, bf16[2,256,8,128]{1,3,2,0:T(8,128)(2,1)S(1)}, u32[]{:S(2)}, u32[]{:S(2)}) %collective-permute-start.2) | collective-permute-done | bytes 1048608 | tf_op jit(solution)/shard_map/while/body/eval_jaxpr/ppermute | solution.py:24
  931.0 148.6 %all-reduce.14.cloned.1.call-done = f32[1,9,256,256]{3,2,1,0:T(8,128)} async-done(((f32[1,9,256,256]{3,2,1,0:T(8,128)}), f32[1,9,256,256]{3,2,1,0:T(8,128)}) %all-reduce.14.cloned.1.call-update) | async-done | bytes 2359312 | tf_op jit(solution)/shard_map/psum | solution.py:111
  (389 shorter events, 414.1 us)
Async XLA Ops:
  7.2 1072.4 %all-reduce.14.cloned.1.call-start = ((), (), s32[]{:S(2)}) async-start(), calls=%async_computation | async-start | bytes 4718592 | tf_op jit(solution)/shard_map/psum | solution.py:111
  35.8 19.6 %collective-permute-start.2 = (bf16[2,256,8,128]{1,3,2,0:T(8,128)(2,1)}, bf16[2,256,8,128]{1,3,2,0:T(8,128)(2,1)S(1)}, u32[]{:S(2)}, u32[]{:S(2)}) collective-permute-start(bf16[2,256,8,128]{1,3,2,0:T(8,128)(2,1)} %get-tuple-element.335), channel_id=1, source_target_pairs={{16,0},{32,16},{48,32},{64,48},{80,64},{96,80},{112,96},{128,112},... | collective-permute-start | bytes 3145736 | tf_op jit(solution)/shard_map/while/body/eval_jaxpr/ppermute | solution.py:24
  58.4 12.7 %collective-permute-start = (bf16[2,256,1,128]{1,3,2,0:T(8,128)(2,1)}, bf16[2,256,1,128]{1,3,2,0:T(8,128)(2,1)S(1)}, u32[]{:S(2)}, u32[]{:S(2)}) collective-permute-start(bf16[2,256,1,128]{1,3,2,0:T(8,128)(2,1)} %get-tuple-element.333), channel_id=1, source_target_pairs={{1,0},{2,1},{3,2},{4,3},{5,4},{6,5},{7,6},{8,7},{9,8},{10,9},{11,1... | collective-permute-start | bytes 393224 | tf_op jit(solution)/shard_map/while/body/eval_jaxpr/ppermute | solution.py:16
  75.8 19.6 %collective-permute-start.2 = (bf16[2,256,8,128]{1,3,2,0:T(8,128)(2,1)}, bf16[2,256,8,128]{1,3,2,0:T(8,128)(2,1)S(1)}, u32[]{:S(2)}, u32[]{:S(2)}) collective-permute-start(bf16[2,256,8,128]{1,3,2,0:T(8,128)(2,1)} %get-tuple-element.335), channel_id=1, source_target_pairs={{16,0},{32,16},{48,32},{64,48},{80,64},{96,80},{112,96},{128,112},... | collective-permute-start | bytes 3145736 | tf_op jit(solution)/shard_map/while/body/eval_jaxpr/ppermute | solution.py:24
  98.4 12.1 %collective-permute-start = (bf16[2,256,1,128]{1,3,2,0:T(8,128)(2,1)}, bf16[2,256,1,128]{1,3,2,0:T(8,128)(2,1)S(1)}, u32[]{:S(2)}, u32[]{:S(2)}) collective-permute-start(bf16[2,256,1,128]{1,3,2,0:T(8,128)(2,1)} %get-tuple-element.333), channel_id=1, source_target_pairs={{1,0},{2,1},{3,2},{4,3},{5,4},{6,5},{7,6},{8,7},{9,8},{10,9},{11,1... | collective-permute-start | bytes 393224 | tf_op jit(solution)/shard_map/while/body/eval_jaxpr/ppermute | solution.py:16
  115.9 20.5 %collective-permute-start.2 = (bf16[2,256,8,128]{1,3,2,0:T(8,128)(2,1)}, bf16[2,256,8,128]{1,3,2,0:T(8,128)(2,1)S(1)}, u32[]{:S(2)}, u32[]{:S(2)}) collective-permute-start(bf16[2,256,8,128]{1,3,2,0:T(8,128)(2,1)} %get-tuple-element.335), channel_id=1, source_target_pairs={{16,0},{32,16},{48,32},{64,48},{80,64},{96,80},{112,96},{128,112},... | collective-permute-start | bytes 3145736 | tf_op jit(solution)/shard_map/while/body/eval_jaxpr/ppermute | solution.py:24
  139.4 13.3 %collective-permute-start = (bf16[2,256,1,128]{1,3,2,0:T(8,128)(2,1)}, bf16[2,256,1,128]{1,3,2,0:T(8,128)(2,1)S(1)}, u32[]{:S(2)}, u32[]{:S(2)}) collective-permute-start(bf16[2,256,1,128]{1,3,2,0:T(8,128)(2,1)} %get-tuple-element.333), channel_id=1, source_target_pairs={{1,0},{2,1},{3,2},{4,3},{5,4},{6,5},{7,6},{8,7},{9,8},{10,9},{11,1... | collective-permute-start | bytes 393224 | tf_op jit(solution)/shard_map/while/body/eval_jaxpr/ppermute | solution.py:16
  157.3 20.8 %collective-permute-start.2 = (bf16[2,256,8,128]{1,3,2,0:T(8,128)(2,1)}, bf16[2,256,8,128]{1,3,2,0:T(8,128)(2,1)S(1)}, u32[]{:S(2)}, u32[]{:S(2)}) collective-permute-start(bf16[2,256,8,128]{1,3,2,0:T(8,128)(2,1)} %get-tuple-element.335), channel_id=1, source_target_pairs={{16,0},{32,16},{48,32},{64,48},{80,64},{96,80},{112,96},{128,112},... | collective-permute-start | bytes 3145736 | tf_op jit(solution)/shard_map/while/body/eval_jaxpr/ppermute | solution.py:24
  181.1 13.4 %collective-permute-start = (bf16[2,256,1,128]{1,3,2,0:T(8,128)(2,1)}, bf16[2,256,1,128]{1,3,2,0:T(8,128)(2,1)S(1)}, u32[]{:S(2)}, u32[]{:S(2)}) collective-permute-start(bf16[2,256,1,128]{1,3,2,0:T(8,128)(2,1)} %get-tuple-element.333), channel_id=1, source_target_pairs={{1,0},{2,1},{3,2},{4,3},{5,4},{6,5},{7,6},{8,7},{9,8},{10,9},{11,1... | collective-permute-start | bytes 393224 | tf_op jit(solution)/shard_map/while/body/eval_jaxpr/ppermute | solution.py:16
  199.1 23.6 %collective-permute-start.2 = (bf16[2,256,8,128]{1,3,2,0:T(8,128)(2,1)}, bf16[2,256,8,128]{1,3,2,0:T(8,128)(2,1)S(1)}, u32[]{:S(2)}, u32[]{:S(2)}) collective-permute-start(bf16[2,256,8,128]{1,3,2,0:T(8,128)(2,1)} %get-tuple-element.335), channel_id=1, source_target_pairs={{16,0},{32,16},{48,32},{64,48},{80,64},{96,80},{112,96},{128,112},... | collective-permute-start | bytes 3145736 | tf_op jit(solution)/shard_map/while/body/eval_jaxpr/ppermute | solution.py:24
  239.0 23.7 %collective-permute-start.2 = (bf16[2,256,8,128]{1,3,2,0:T(8,128)(2,1)}, bf16[2,256,8,128]{1,3,2,0:T(8,128)(2,1)S(1)}, u32[]{:S(2)}, u32[]{:S(2)}) collective-permute-start(bf16[2,256,8,128]{1,3,2,0:T(8,128)(2,1)} %get-tuple-element.335), channel_id=1, source_target_pairs={{16,0},{32,16},{48,32},{64,48},{80,64},{96,80},{112,96},{128,112},... | collective-permute-start | bytes 3145736 | tf_op jit(solution)/shard_map/while/body/eval_jaxpr/ppermute | solution.py:24
  278.4 23.0 %collective-permute-start.2 = (bf16[2,256,8,128]{1,3,2,0:T(8,128)(2,1)}, bf16[2,256,8,128]{1,3,2,0:T(8,128)(2,1)S(1)}, u32[]{:S(2)}, u32[]{:S(2)}) collective-permute-start(bf16[2,256,8,128]{1,3,2,0:T(8,128)(2,1)} %get-tuple-element.335), channel_id=1, source_target_pairs={{16,0},{32,16},{48,32},{64,48},{80,64},{96,80},{112,96},{128,112},... | collective-permute-start | bytes 3145736 | tf_op jit(solution)/shard_map/while/body/eval_jaxpr/ppermute | solution.py:24
  317.6 22.9 %collective-permute-start.2 = (bf16[2,256,8,128]{1,3,2,0:T(8,128)(2,1)}, bf16[2,256,8,128]{1,3,2,0:T(8,128)(2,1)S(1)}, u32[]{:S(2)}, u32[]{:S(2)}) collective-permute-start(bf16[2,256,8,128]{1,3,2,0:T(8,128)(2,1)} %get-tuple-element.335), channel_id=1, source_target_pairs={{16,0},{32,16},{48,32},{64,48},{80,64},{96,80},{112,96},{128,112},... | collective-permute-start | bytes 3145736 | tf_op jit(solution)/shard_map/while/body/eval_jaxpr/ppermute | solution.py:24
  356.7 22.7 %collective-permute-start.2 = (bf16[2,256,8,128]{1,3,2,0:T(8,128)(2,1)}, bf16[2,256,8,128]{1,3,2,0:T(8,128)(2,1)S(1)}, u32[]{:S(2)}, u32[]{:S(2)}) collective-permute-start(bf16[2,256,8,128]{1,3,2,0:T(8,128)(2,1)} %get-tuple-element.335), channel_id=1, source_target_pairs={{16,0},{32,16},{48,32},{64,48},{80,64},{96,80},{112,96},{128,112},... | collective-permute-start | bytes 3145736 | tf_op jit(solution)/shard_map/while/body/eval_jaxpr/ppermute | solution.py:24
  395.7 22.7 %collective-permute-start.2 = (bf16[2,256,8,128]{1,3,2,0:T(8,128)(2,1)}, bf16[2,256,8,128]{1,3,2,0:T(8,128)(2,1)S(1)}, u32[]{:S(2)}, u32[]{:S(2)}) collective-permute-start(bf16[2,256,8,128]{1,3,2,0:T(8,128)(2,1)} %get-tuple-element.335), channel_id=1, source_target_pairs={{16,0},{32,16},{48,32},{64,48},{80,64},{96,80},{112,96},{128,112},... | collective-permute-start | bytes 3145736 | tf_op jit(solution)/shard_map/while/body/eval_jaxpr/ppermute | solution.py:24
  434.8 23.9 %collective-permute-start.2 = (bf16[2,256,8,128]{1,3,2,0:T(8,128)(2,1)}, bf16[2,256,8,128]{1,3,2,0:T(8,128)(2,1)S(1)}, u32[]{:S(2)}, u32[]{:S(2)}) collective-permute-start(bf16[2,256,8,128]{1,3,2,0:T(8,128)(2,1)} %get-tuple-element.335), channel_id=1, source_target_pairs={{16,0},{32,16},{48,32},{64,48},{80,64},{96,80},{112,96},{128,112},... | collective-permute-start | bytes 3145736 | tf_op jit(solution)/shard_map/while/body/eval_jaxpr/ppermute | solution.py:24
  461.8 10.2 collective-permute-start
  475.8 23.4 %collective-permute-start.2 = (bf16[2,256,8,128]{1,3,2,0:T(8,128)(2,1)}, bf16[2,256,8,128]{1,3,2,0:T(8,128)(2,1)S(1)}, u32[]{:S(2)}, u32[]{:S(2)}) collective-permute-start(bf16[2,256,8,128]{1,3,2,0:T(8,128)(2,1)} %get-tuple-element.335), channel_id=1, source_target_pairs={{16,0},{32,16},{48,32},{64,48},{80,64},{96,80},{112,96},{128,112},... | collective-permute-start | bytes 3145736 | tf_op jit(solution)/shard_map/while/body/eval_jaxpr/ppermute | solution.py:24
  516.2 23.3 %collective-permute-start.2 = (bf16[2,256,8,128]{1,3,2,0:T(8,128)(2,1)}, bf16[2,256,8,128]{1,3,2,0:T(8,128)(2,1)S(1)}, u32[]{:S(2)}, u32[]{:S(2)}) collective-permute-start(bf16[2,256,8,128]{1,3,2,0:T(8,128)(2,1)} %get-tuple-element.335), channel_id=1, source_target_pairs={{16,0},{32,16},{48,32},{64,48},{80,64},{96,80},{112,96},{128,112},... | collective-permute-start | bytes 3145736 | tf_op jit(solution)/shard_map/while/body/eval_jaxpr/ppermute | solution.py:24
  542.5 10.2 collective-permute-start
  556.5 23.1 %collective-permute-start.2 = (bf16[2,256,8,128]{1,3,2,0:T(8,128)(2,1)}, bf16[2,256,8,128]{1,3,2,0:T(8,128)(2,1)S(1)}, u32[]{:S(2)}, u32[]{:S(2)}) collective-permute-start(bf16[2,256,8,128]{1,3,2,0:T(8,128)(2,1)} %get-tuple-element.335), channel_id=1, source_target_pairs={{16,0},{32,16},{48,32},{64,48},{80,64},{96,80},{112,96},{128,112},... | collective-permute-start | bytes 3145736 | tf_op jit(solution)/shard_map/while/body/eval_jaxpr/ppermute | solution.py:24
  596.5 269.6 %collective-permute-start.2 = (bf16[2,256,8,128]{1,3,2,0:T(8,128)(2,1)}, bf16[2,256,8,128]{1,3,2,0:T(8,128)(2,1)S(1)}, u32[]{:S(2)}, u32[]{:S(2)}) collective-permute-start(bf16[2,256,8,128]{1,3,2,0:T(8,128)(2,1)} %get-tuple-element.335), channel_id=1, source_target_pairs={{16,0},{32,16},{48,32},{64,48},{80,64},{96,80},{112,96},{128,112},... | collective-permute-start | bytes 3145736 | tf_op jit(solution)/shard_map/while/body/eval_jaxpr/ppermute | solution.py:24
  869.2 10.4 collective-permute-start
  901.5 22.1 %collective-permute-start.2 = (bf16[2,256,8,128]{1,3,2,0:T(8,128)(2,1)}, bf16[2,256,8,128]{1,3,2,0:T(8,128)(2,1)S(1)}, u32[]{:S(2)}, u32[]{:S(2)}) collective-permute-start(bf16[2,256,8,128]{1,3,2,0:T(8,128)(2,1)} %get-tuple-element.335), channel_id=1, source_target_pairs={{16,0},{32,16},{48,32},{64,48},{80,64},{96,80},{112,96},{128,112},... | collective-permute-start | bytes 3145736 | tf_op jit(solution)/shard_map/while/body/eval_jaxpr/ppermute | solution.py:24
  (94 other events, 797.1 us)
Sparse Core Ops, SparseCore 0:
  928.4 151.1 all-reduce.13
where the time goes:
time: 1090 us
  waiting for transfers between devices  686 us (63%)
  starting transfers between devices  144 us (13%)
  other arithmetic  122 us (11%)
  local copies, waits for them, and re-layouts  95 us (9%)
  matrix products  17.4 us (2%)
  between operations  14.1 us (1%)
  loops' own time  11.6 us (1%)
    ppermute x16, waiting for transfers between devices, from_behind(): return lax.ppermute(block, axis, route)  504 us
    psum x1, waiting for transfers between devices, per_device(): weight_grad = lax.psum(kernel_acc * scale, 'tile')  149 us
    ppermute x17, starting transfers between devices, padded_2(): lax.ppermute(lax.slice_in_dim(block, 0, width, axis=dim), axis, backward)  89.3 us
    another operation x31, local copies, waits for them, and re-layouts  41.5 us
    add x16, other arithmetic, one_tick(): kernel_acc = kernel_acc + partial_k  39.1 us
    select_n x16, other arithmetic, one_tick(): grads = jnp.where(valid, lowered, old_grads)  39 us
    ppermute x17, starting transfers between devices, padded_2(): lax.ppermute(lax.slice_in_dim(block, block.shape[dim] - width, None, axis...  33.7 us
    ppermute x17, waiting for transfers between devices, padded_2(): lax.ppermute(lax.slice_in_dim(block, 0, width, axis=dim), axis, backward)  28.9 us
  transfers between devices with their start and end apart: 51, of which 39 were waited for; matrix products, arithmetic and copies ran while one was open for 9% of the time, Pallas kernels for 0%

commit v1 on v0

--- a/solution.py
+++ b/solution.py
@@ -2,6 +2,12 @@
 import jax.numpy as jnp
 from jax import lax
 from jax.sharding import PartitionSpec as P
+
+
+def add_all(shard, axis):
+    parts = lax.all_gather(shard, axis, axis=0, tiled=False)
+    acc = parts.sum(axis=0)
+    return acc
 
 
 def padded_2(block, sides, width):
@@ -108,7 +114,7 @@
     final, unused = lax.scan(one_tick, initial, jnp.arange(ticks, dtype=jnp.int32))
     grads = final[1]
     kernel_acc = final[2]
-    weight_grad = lax.psum(kernel_acc * scale, "tile")
+    weight_grad = add_all(kernel_acc * scale, "tile")
     return (grads[None], weight_grad[None])
 
 

time: 1090 us -> 1170 us (1.073)
  waiting for transfers between devices: 686 us -> 750 us
  other arithmetic: 122 us -> 135 us
    all_gather x0 -> x1, waiting for transfers between devices: none -> 211 us  [add_all(): parts = lax.all_gather(shard, axis, axis=0, tiled=False)]
    psum x1 -> x0, waiting for transfers between devices: 149 us -> none  [per_device(): weight_grad = lax.psum(kernel_acc * scale, 'tile')]
    reduce_sum x0 -> x1, other arithmetic: none -> 14.9 us  [add_all(): acc = parts.sum(axis=0)]
  transfers between devices with their start and end apart: 51 -> 51, of which waited for: 39 -> 39; matrix products, arithmetic and copies ran while one was open for 9% -> 8% of each run, Pallas kernels for 0% -> 0%
where the time goes in v1:
time: 1170 us
  waiting for transfers between devices  750 us (64%)
  starting transfers between devices  143 us (12%)
  other arithmetic  135 us (12%)
  local copies, waits for them, and re-layouts  97.4 us (8%)
  matrix products  17.4 us (1%)
  between operations  14.1 us (1%)
  loops' own time  12.5 us (1%)
    ppermute x16, waiting for transfers between devices, from_behind(): return lax.ppermute(block, axis, route)  507 us
    all_gather x1, waiting for transfers between devices, add_all(): parts = lax.all_gather(shard, axis, axis=0, tiled=False)  211 us
    ppermute x17, starting transfers between devices, padded_2(): lax.ppermute(lax.slice_in_dim(block, 0, width, axis=dim), axis, backward)  89.4 us
    another operation x31, local copies, waits for them, and re-layouts  41.6 us
    add x16, other arithmetic, one_tick(): kernel_acc = kernel_acc + partial_k  39.1 us
    select_n x16, other arithmetic, one_tick(): grads = jnp.where(valid, lowered, old_grads)  38.8 us
    ppermute x17, starting transfers between devices, padded_2(): lax.ppermute(lax.slice_in_dim(block, block.shape[dim] - width, None, axis...  33.5 us
    ppermute x17, waiting for transfers between devices, padded_2(): lax.ppermute(lax.slice_in_dim(block, 0, width, axis=dim), axis, backward)  27.5 us
  transfers between devices with their start and end apart: 51, of which 39 were waited for; matrix products, arithmetic and copies ran while one was open for 8% of the time, Pallas kernels for 0%

profile of v1, /device:TPU:1, one launch (start us, length us, event | category | flops | bytes accessed | tf_op | source)
XLA Modules:
  0.0 1170.3 jit_solution(12365275682039466058)
XLA Ops:
  22.9 904.1 %while.17 = (s32[]{:T(128)}, bf16[2,256,8,128]{1,3,2,0:T(8,128)(2,1)}, bf16[2,256,8,128]{1,3,2,0:T(8,128)(2,1)}, f32[9,256,256]{1,2,0:T(8,128)}, s32[16]{0:T(128...) while((s32[]{:T(128)}, ...), condition=%wide.region_3.4_spmd.clone, body=%wide.region_0.3_spmd.clone.sunk | while | flops 4842192896 | bytes 153502240 | solution.py:114
  40.7 13.8 %collective-permute-done.2 = bf16[2,256,8,128]{1,3,2,0:T(8,128)(2,1)S(1)} collective-permute-done((bf16[2,256,8,128]{1,3,2,0:T(8,128)(2,1)}, bf16[2,256,8,128]{1,3,2,0:T(8,128)(2,1)S(1)}, u32[]{:S(2)}, u32[]{:S(2)}) %collective-permute-start.2) | collective-permute-done | bytes 1048608 | tf_op jit(solution)/shard_map/while/body/eval_jaxpr/ppermute | solution.py:30
  57.5 8.1 collective-permute-start
  81.2 13.3 %collective-permute-done.2 = bf16[2,256,8,128]{1,3,2,0:T(8,128)(2,1)S(1)} collective-permute-done((bf16[2,256,8,128]{1,3,2,0:T(8,128)(2,1)}, bf16[2,256,8,128]{1,3,2,0:T(8,128)(2,1)S(1)}, u32[]{:S(2)}, u32[]{:S(2)}) %collective-permute-start.2) | collective-permute-done | bytes 1048608 | tf_op jit(solution)/shard_map/while/body/eval_jaxpr/ppermute | solution.py:30
  97.6 8.1 collective-permute-start
  121.3 14.2 %collective-permute-done.2 = bf16[2,256,8,128]{1,3,2,0:T(8,128)(2,1)S(1)} collective-permute-done((bf16[2,256,8,128]{1,3,2,0:T(8,128)(2,1)}, bf16[2,256,8,128]{1,3,2,0:T(8,128)(2,1)S(1)}, u32[]{:S(2)}, u32[]{:S(2)}) %collective-permute-start.2) | collective-permute-done | bytes 1048608 | tf_op jit(solution)/shard_map/while/body/eval_jaxpr/ppermute | solution.py:30
  138.6 7.8 collective-permute-start
  162.7 14.4 %collective-permute-done.2 = bf16[2,256,8,128]{1,3,2,0:T(8,128)(2,1)S(1)} collective-permute-done((bf16[2,256,8,128]{1,3,2,0:T(8,128)(2,1)}, bf16[2,256,8,128]{1,3,2,0:T(8,128)(2,1)S(1)}, u32[]{:S(2)}, u32[]{:S(2)}) %collective-permute-start.2) | collective-permute-done | bytes 1048608 | tf_op jit(solution)/shard_map/while/body/eval_jaxpr/ppermute | solution.py:30
  180.1 7.0 collective-permute-start
  204.4 17.3 %collective-permute-done.2 = bf16[2,256,8,128]{1,3,2,0:T(8,128)(2,1)S(1)} collective-permute-done((bf16[2,256,8,128]{1,3,2,0:T(8,128)(2,1)}, bf16[2,256,8,128]{1,3,2,0:T(8,128)(2,1)S(1)}, u32[]{:S(2)}, u32[]{:S(2)}) %collective-permute-start.2) | collective-permute-done | bytes 1048608 | tf_op jit(solution)/shard_map/while/body/eval_jaxpr/ppermute | solution.py:30
  244.4 17.5 %collective-permute-done.2 = bf16[2,256,8,128]{1,3,2,0:T(8,128)(2,1)S(1)} collective-permute-done((bf16[2,256,8,128]{1,3,2,0:T(8,128)(2,1)}, bf16[2,256,8,128]{1,3,2,0:T(8,128)(2,1)S(1)}, u32[]{:S(2)}, u32[]{:S(2)}) %collective-permute-start.2) | collective-permute-done | bytes 1048608 | tf_op jit(solution)/shard_map/while/body/eval_jaxpr/ppermute | solution.py:30
  283.7 16.7 %collective-permute-done.2 = bf16[2,256,8,128]{1,3,2,0:T(8,128)(2,1)S(1)} collective-permute-done((bf16[2,256,8,128]{1,3,2,0:T(8,128)(2,1)}, bf16[2,256,8,128]{1,3,2,0:T(8,128)(2,1)S(1)}, u32[]{:S(2)}, u32[]{:S(2)}) %collective-permute-start.2) | collective-permute-done | bytes 1048608 | tf_op jit(solution)/shard_map/while/body/eval_jaxpr/ppermute | solution.py:30
  323.0 16.6 %collective-permute-done.2 = bf16[2,256,8,128]{1,3,2,0:T(8,128)(2,1)S(1)} collective-permute-done((bf16[2,256,8,128]{1,3,2,0:T(8,128)(2,1)}, bf16[2,256,8,128]{1,3,2,0:T(8,128)(2,1)S(1)}, u32[]{:S(2)}, u32[]{:S(2)}) %collective-permute-start.2) | collective-permute-done | bytes 1048608 | tf_op jit(solution)/shard_map/while/body/eval_jaxpr/ppermute | solution.py:30
  362.1 16.5 %collective-permute-done.2 = bf16[2,256,8,128]{1,3,2,0:T(8,128)(2,1)S(1)} collective-permute-done((bf16[2,256,8,128]{1,3,2,0:T(8,128)(2,1)}, bf16[2,256,8,128]{1,3,2,0:T(8,128)(2,1)S(1)}, u32[]{:S(2)}, u32[]{:S(2)}) %collective-permute-start.2) | collective-permute-done | bytes 1048608 | tf_op jit(solution)/shard_map/while/body/eval_jaxpr/ppermute | solution.py:30
  401.1 16.5 %collective-permute-done.2 = bf16[2,256,8,128]{1,3,2,0:T(8,128)(2,1)S(1)} collective-permute-done((bf16[2,256,8,128]{1,3,2,0:T(8,128)(2,1)}, bf16[2,256,8,128]{1,3,2,0:T(8,128)(2,1)S(1)}, u32[]{:S(2)}, u32[]{:S(2)}) %collective-permute-start.2) | collective-permute-done | bytes 1048608 | tf_op jit(solution)/shard_map/while/body/eval_jaxpr/ppermute | solution.py:30
  440.3 17.7 %collective-permute-done.2 = bf16[2,256,8,128]{1,3,2,0:T(8,128)(2,1)S(1)} collective-permute-done((bf16[2,256,8,128]{1,3,2,0:T(8,128)(2,1)}, bf16[2,256,8,128]{1,3,2,0:T(8,128)(2,1)S(1)}, u32[]{:S(2)}, u32[]{:S(2)}) %collective-permute-start.2) | collective-permute-done | bytes 1048608 | tf_op jit(solution)/shard_map/while/body/eval_jaxpr/ppermute | solution.py:30
  481.2 17.2 %collective-permute-done.2 = bf16[2,256,8,128]{1,3,2,0:T(8,128)(2,1)S(1)} collective-permute-done((bf16[2,256,8,128]{1,3,2,0:T(8,128)(2,1)}, bf16[2,256,8,128]{1,3,2,0:T(8,128)(2,1)S(1)}, u32[]{:S(2)}, u32[]{:S(2)}) %collective-permute-start.2) | collective-permute-done | bytes 1048608 | tf_op jit(solution)/shard_map/while/body/eval_jaxpr/ppermute | solution.py:30
  521.7 17.0 %collective-permute-done.2 = bf16[2,256,8,128]{1,3,2,0:T(8,128)(2,1)S(1)} collective-permute-done((bf16[2,256,8,128]{1,3,2,0:T(8,128)(2,1)}, bf16[2,256,8,128]{1,3,2,0:T(8,128)(2,1)S(1)}, u32[]{:S(2)}, u32[]{:S(2)}) %collective-permute-start.2) | collective-permute-done | bytes 1048608 | tf_op jit(solution)/shard_map/while/body/eval_jaxpr/ppermute | solution.py:30
  562.0 16.8 %collective-permute-done.2 = bf16[2,256,8,128]{1,3,2,0:T(8,128)(2,1)S(1)} collective-permute-done((bf16[2,256,8,128]{1,3,2,0:T(8,128)(2,1)}, bf16[2,256,8,128]{1,3,2,0:T(8,128)(2,1)S(1)}, u32[]{:S(2)}, u32[]{:S(2)}) %collective-permute-start.2) | collective-permute-done | bytes 1048608 | tf_op jit(solution)/shard_map/while/body/eval_jaxpr/ppermute | solution.py:30
  602.0 266.2 %collective-permute-done.2 = bf16[2,256,8,128]{1,3,2,0:T(8,128)(2,1)S(1)} collective-permute-done((bf16[2,256,8,128]{1,3,2,0:T(8,128)(2,1)}, bf16[2,256,8,128]{1,3,2,0:T(8,128)(2,1)S(1)}, u32[]{:S(2)}, u32[]{:S(2)}) %collective-permute-start.2) | collective-permute-done | bytes 1048608 | tf_op jit(solution)/shard_map/while/body/eval_jaxpr/ppermute | solution.py:30
  882.8 21.1 %conditional.3 = (bf16[2,256,8,128]{1,3,2,0:T(8,128)(2,1)}, f32[9,256,256]{1,2,0:T(8,128)}) conditional(s32[]{:T(128)} %convert_element_type.29, () %tuple.65, (bf16[2,256,8,128]{1,3,2,0:T(8,128)(2,1)S(1)}, bf16[2,256,10,128]{1,3,2,0:T(8,128)(2,1)S(1)}, bf16[9,256,256]{2,1,0:T(8,128)(2,1)}, f32[2,256,8,128]{1,3,2,0:T(8,128)S(1)}, ...), branch_computations={%region_1.1_spmd, %region_2.2_spmd} | conditional | flops 4838129664 | bytes 100286512 | solution.py:99
  910.4 15.6 %collective-permute-done.2 = bf16[2,256,8,128]{1,3,2,0:T(8,128)(2,1)S(1)} collective-permute-done((bf16[2,256,8,128]{1,3,2,0:T(8,128)(2,1)}, bf16[2,256,8,128]{1,3,2,0:T(8,128)(2,1)S(1)}, u32[]{:S(2)}, u32[]{:S(2)}) %collective-permute-start.2) | collective-permute-done | bytes 1048608 | tf_op jit(solution)/shard_map/while/body/eval_jaxpr/ppermute | solution.py:30
  933.3 211.2 %all-gather.3.cloned.1.call-done = f32[144,256,256]{2,1,0:T(8,128)} async-done(((f32[9,256,256]{2,1,0:T(8,128)}), f32[144,256,256]{2,1,0:T(8,128)}) %all-gather.3.cloned.1.call-update) | async-done | bytes 37748752 | tf_op jit(solution)/shard_map/all_gather | solution.py:8
  1144.5 14.9 %reduce_sum.9 = f32[9,256,256]{2,1,0:T(8,128)} reduce(f32[16,9,256,256]{3,2,1,0:T(8,128)} %bitcast.173, f32[]{:T(128)} %constant.33.clone.1), dimensions={0}, to_apply=%region_4.5 | reduce | flops 8847360 | bytes 40108036 | tf_op jit(solution)/shard_map/reduce_sum | solution.py:9
  (389 shorter events, 420.2 us)
Async XLA Ops:
  7.2 1137.4 %all-gather.3.cloned.1.call-start = ((), (), s32[]{:S(2)}) async-start(), calls=%async_computation | async-start | bytes 40108032 | tf_op jit(solution)/shard_map/all_gather | solution.py:8
  34.9 19.6 %collective-permute-start.2 = (bf16[2,256,8,128]{1,3,2,0:T(8,128)(2,1)}, bf16[2,256,8,128]{1,3,2,0:T(8,128)(2,1)S(1)}, u32[]{:S(2)}, u32[]{:S(2)}) collective-permute-start(bf16[2,256,8,128]{1,3,2,0:T(8,128)(2,1)} %get-tuple-element.349), channel_id=1, source_target_pairs={{16,0},{32,16},{48,32},{64,48},{80,64},{96,80},{112,96},{128,112},... | collective-permute-start | bytes 3145736 | tf_op jit(solution)/shard_map/while/body/eval_jaxpr/ppermute | solution.py:30
  57.5 12.7 %collective-permute-start = (bf16[2,256,1,128]{1,3,2,0:T(8,128)(2,1)}, bf16[2,256,1,128]{1,3,2,0:T(8,128)(2,1)S(1)}, u32[]{:S(2)}, u32[]{:S(2)}) collective-permute-start(bf16[2,256,1,128]{1,3,2,0:T(8,128)(2,1)} %get-tuple-element.347), channel_id=1, source_target_pairs={{1,0},{2,1},{3,2},{4,3},{5,4},{6,5},{7,6},{8,7},{9,8},{10,9},{11,1... | collective-permute-start | bytes 393224 | tf_op jit(solution)/shard_map/while/body/eval_jaxpr/ppermute | solution.py:22
  74.9 19.6 %collective-permute-start.2 = (bf16[2,256,8,128]{1,3,2,0:T(8,128)(2,1)}, bf16[2,256,8,128]{1,3,2,0:T(8,128)(2,1)S(1)}, u32[]{:S(2)}, u32[]{:S(2)}) collective-permute-start(bf16[2,256,8,128]{1,3,2,0:T(8,128)(2,1)} %get-tuple-element.349), channel_id=1, source_target_pairs={{16,0},{32,16},{48,32},{64,48},{80,64},{96,80},{112,96},{128,112},... | collective-permute-start | bytes 3145736 | tf_op jit(solution)/shard_map/while/body/eval_jaxpr/ppermute | solution.py:30
  97.6 12.0 %collective-permute-start = (bf16[2,256,1,128]{1,3,2,0:T(8,128)(2,1)}, bf16[2,256,1,128]{1,3,2,0:T(8,128)(2,1)S(1)}, u32[]{:S(2)}, u32[]{:S(2)}) collective-permute-start(bf16[2,256,1,128]{1,3,2,0:T(8,128)(2,1)} %get-tuple-element.347), channel_id=1, source_target_pairs={{1,0},{2,1},{3,2},{4,3},{5,4},{6,5},{7,6},{8,7},{9,8},{10,9},{11,1... | collective-permute-start | bytes 393224 | tf_op jit(solution)/shard_map/while/body/eval_jaxpr/ppermute | solution.py:22
  115.1 20.5 %collective-permute-start.2 = (bf16[2,256,8,128]{1,3,2,0:T(8,128)(2,1)}, bf16[2,256,8,128]{1,3,2,0:T(8,128)(2,1)S(1)}, u32[]{:S(2)}, u32[]{:S(2)}) collective-permute-start(bf16[2,256,8,128]{1,3,2,0:T(8,128)(2,1)} %get-tuple-element.349), channel_id=1, source_target_pairs={{16,0},{32,16},{48,32},{64,48},{80,64},{96,80},{112,96},{128,112},... | collective-permute-start | bytes 3145736 | tf_op jit(solution)/shard_map/while/body/eval_jaxpr/ppermute | solution.py:30
  138.6 13.2 %collective-permute-start = (bf16[2,256,1,128]{1,3,2,0:T(8,128)(2,1)}, bf16[2,256,1,128]{1,3,2,0:T(8,128)(2,1)S(1)}, u32[]{:S(2)}, u32[]{:S(2)}) collective-permute-start(bf16[2,256,1,128]{1,3,2,0:T(8,128)(2,1)} %get-tuple-element.347), channel_id=1, source_target_pairs={{1,0},{2,1},{3,2},{4,3},{5,4},{6,5},{7,6},{8,7},{9,8},{10,9},{11,1... | collective-permute-start | bytes 393224 | tf_op jit(solution)/shard_map/while/body/eval_jaxpr/ppermute | solution.py:22
  156.4 20.7 %collective-permute-start.2 = (bf16[2,256,8,128]{1,3,2,0:T(8,128)(2,1)}, bf16[2,256,8,128]{1,3,2,0:T(8,128)(2,1)S(1)}, u32[]{:S(2)}, u32[]{:S(2)}) collective-permute-start(bf16[2,256,8,128]{1,3,2,0:T(8,128)(2,1)} %get-tuple-element.349), channel_id=1, source_target_pairs={{16,0},{32,16},{48,32},{64,48},{80,64},{96,80},{112,96},{128,112},... | collective-permute-start | bytes 3145736 | tf_op jit(solution)/shard_map/while/body/eval_jaxpr/ppermute | solution.py:30
  180.1 13.5 %collective-permute-start = (bf16[2,256,1,128]{1,3,2,0:T(8,128)(2,1)}, bf16[2,256,1,128]{1,3,2,0:T(8,128)(2,1)S(1)}, u32[]{:S(2)}, u32[]{:S(2)}) collective-permute-start(bf16[2,256,1,128]{1,3,2,0:T(8,128)(2,1)} %get-tuple-element.347), channel_id=1, source_target_pairs={{1,0},{2,1},{3,2},{4,3},{5,4},{6,5},{7,6},{8,7},{9,8},{10,9},{11,1... | collective-permute-start | bytes 393224 | tf_op jit(solution)/shard_map/while/body/eval_jaxpr/ppermute | solution.py:22
  198.2 23.6 %collective-permute-start.2 = (bf16[2,256,8,128]{1,3,2,0:T(8,128)(2,1)}, bf16[2,256,8,128]{1,3,2,0:T(8,128)(2,1)S(1)}, u32[]{:S(2)}, u32[]{:S(2)}) collective-permute-start(bf16[2,256,8,128]{1,3,2,0:T(8,128)(2,1)} %get-tuple-element.349), channel_id=1, source_target_pairs={{16,0},{32,16},{48,32},{64,48},{80,64},{96,80},{112,96},{128,112},... | collective-permute-start | bytes 3145736 | tf_op jit(solution)/shard_map/while/body/eval_jaxpr/ppermute | solution.py:30
  238.1 23.7 %collective-permute-start.2 = (bf16[2,256,8,128]{1,3,2,0:T(8,128)(2,1)}, bf16[2,256,8,128]{1,3,2,0:T(8,128)(2,1)S(1)}, u32[]{:S(2)}, u32[]{:S(2)}) collective-permute-start(bf16[2,256,8,128]{1,3,2,0:T(8,128)(2,1)} %get-tuple-element.349), channel_id=1, source_target_pairs={{16,0},{32,16},{48,32},{64,48},{80,64},{96,80},{112,96},{128,112},... | collective-permute-start | bytes 3145736 | tf_op jit(solution)/shard_map/while/body/eval_jaxpr/ppermute | solution.py:30
  277.5 23.0 %collective-permute-start.2 = (bf16[2,256,8,128]{1,3,2,0:T(8,128)(2,1)}, bf16[2,256,8,128]{1,3,2,0:T(8,128)(2,1)S(1)}, u32[]{:S(2)}, u32[]{:S(2)}) collective-permute-start(bf16[2,256,8,128]{1,3,2,0:T(8,128)(2,1)} %get-tuple-element.349), channel_id=1, source_target_pairs={{16,0},{32,16},{48,32},{64,48},{80,64},{96,80},{112,96},{128,112},... | collective-permute-start | bytes 3145736 | tf_op jit(solution)/shard_map/while/body/eval_jaxpr/ppermute | solution.py:30
  316.7 22.9 %collective-permute-start.2 = (bf16[2,256,8,128]{1,3,2,0:T(8,128)(2,1)}, bf16[2,256,8,128]{1,3,2,0:T(8,128)(2,1)S(1)}, u32[]{:S(2)}, u32[]{:S(2)}) collective-permute-start(bf16[2,256,8,128]{1,3,2,0:T(8,128)(2,1)} %get-tuple-element.349), channel_id=1, source_target_pairs={{16,0},{32,16},{48,32},{64,48},{80,64},{96,80},{112,96},{128,112},... | collective-permute-start | bytes 3145736 | tf_op jit(solution)/shard_map/while/body/eval_jaxpr/ppermute | solution.py:30
  355.9 22.7 %collective-permute-start.2 = (bf16[2,256,8,128]{1,3,2,0:T(8,128)(2,1)}, bf16[2,256,8,128]{1,3,2,0:T(8,128)(2,1)S(1)}, u32[]{:S(2)}, u32[]{:S(2)}) collective-permute-start(bf16[2,256,8,128]{1,3,2,0:T(8,128)(2,1)} %get-tuple-element.349), channel_id=1, source_target_pairs={{16,0},{32,16},{48,32},{64,48},{80,64},{96,80},{112,96},{128,112},... | collective-permute-start | bytes 3145736 | tf_op jit(solution)/shard_map/while/body/eval_jaxpr/ppermute | solution.py:30
  394.9 22.7 %collective-permute-start.2 = (bf16[2,256,8,128]{1,3,2,0:T(8,128)(2,1)}, bf16[2,256,8,128]{1,3,2,0:T(8,128)(2,1)S(1)}, u32[]{:S(2)}, u32[]{:S(2)}) collective-permute-start(bf16[2,256,8,128]{1,3,2,0:T(8,128)(2,1)} %get-tuple-element.349), channel_id=1, source_target_pairs={{16,0},{32,16},{48,32},{64,48},{80,64},{96,80},{112,96},{128,112},... | collective-permute-start | bytes 3145736 | tf_op jit(solution)/shard_map/while/body/eval_jaxpr/ppermute | solution.py:30
  434.0 23.9 %collective-permute-start.2 = (bf16[2,256,8,128]{1,3,2,0:T(8,128)(2,1)}, bf16[2,256,8,128]{1,3,2,0:T(8,128)(2,1)S(1)}, u32[]{:S(2)}, u32[]{:S(2)}) collective-permute-start(bf16[2,256,8,128]{1,3,2,0:T(8,128)(2,1)} %get-tuple-element.349), channel_id=1, source_target_pairs={{16,0},{32,16},{48,32},{64,48},{80,64},{96,80},{112,96},{128,112},... | collective-permute-start | bytes 3145736 | tf_op jit(solution)/shard_map/while/body/eval_jaxpr/ppermute | solution.py:30
  475.0 23.4 %collective-permute-start.2 = (bf16[2,256,8,128]{1,3,2,0:T(8,128)(2,1)}, bf16[2,256,8,128]{1,3,2,0:T(8,128)(2,1)S(1)}, u32[]{:S(2)}, u32[]{:S(2)}) collective-permute-start(bf16[2,256,8,128]{1,3,2,0:T(8,128)(2,1)} %get-tuple-element.349), channel_id=1, source_target_pairs={{16,0},{32,16},{48,32},{64,48},{80,64},{96,80},{112,96},{128,112},... | collective-permute-start | bytes 3145736 | tf_op jit(solution)/shard_map/while/body/eval_jaxpr/ppermute | solution.py:30
  515.4 23.3 %collective-permute-start.2 = (bf16[2,256,8,128]{1,3,2,0:T(8,128)(2,1)}, bf16[2,256,8,128]{1,3,2,0:T(8,128)(2,1)S(1)}, u32[]{:S(2)}, u32[]{:S(2)}) collective-permute-start(bf16[2,256,8,128]{1,3,2,0:T(8,128)(2,1)} %get-tuple-element.349), channel_id=1, source_target_pairs={{16,0},{32,16},{48,32},{64,48},{80,64},{96,80},{112,96},{128,112},... | collective-permute-start | bytes 3145736 | tf_op jit(solution)/shard_map/while/body/eval_jaxpr/ppermute | solution.py:30
  541.7 10.2 collective-permute-start
  555.7 23.1 %collective-permute-start.2 = (bf16[2,256,8,128]{1,3,2,0:T(8,128)(2,1)}, bf16[2,256,8,128]{1,3,2,0:T(8,128)(2,1)S(1)}, u32[]{:S(2)}, u32[]{:S(2)}) collective-permute-start(bf16[2,256,8,128]{1,3,2,0:T(8,128)(2,1)} %get-tuple-element.349), channel_id=1, source_target_pairs={{16,0},{32,16},{48,32},{64,48},{80,64},{96,80},{112,96},{128,112},... | collective-permute-start | bytes 3145736 | tf_op jit(solution)/shard_map/while/body/eval_jaxpr/ppermute | solution.py:30
  581.8 10.2 collective-permute-start
  595.8 272.5 %collective-permute-start.2 = (bf16[2,256,8,128]{1,3,2,0:T(8,128)(2,1)}, bf16[2,256,8,128]{1,3,2,0:T(8,128)(2,1)S(1)}, u32[]{:S(2)}, u32[]{:S(2)}) collective-permute-start(bf16[2,256,8,128]{1,3,2,0:T(8,128)(2,1)} %get-tuple-element.349), channel_id=1, source_target_pairs={{16,0},{32,16},{48,32},{64,48},{80,64},{96,80},{112,96},{128,112},... | collective-permute-start | bytes 3145736 | tf_op jit(solution)/shard_map/while/body/eval_jaxpr/ppermute | solution.py:30
  871.2 10.4 collective-permute-start
  903.8 22.1 %collective-permute-start.2 = (bf16[2,256,8,128]{1,3,2,0:T(8,128)(2,1)}, bf16[2,256,8,128]{1,3,2,0:T(8,128)(2,1)S(1)}, u32[]{:S(2)}, u32[]{:S(2)}) collective-permute-start(bf16[2,256,8,128]{1,3,2,0:T(8,128)(2,1)} %get-tuple-element.349), channel_id=1, source_target_pairs={{16,0},{32,16},{48,32},{64,48},{80,64},{96,80},{112,96},{128,112},... | collective-permute-start | bytes 3145736 | tf_op jit(solution)/shard_map/while/body/eval_jaxpr/ppermute | solution.py:30
  (93 other events, 790.2 us)
Sparse Core Ops, SparseCore 0:
  930.8 213.6 all-gather.2
